TPU v7x, 32 devices: a whole 2x2x4 slice. The times are simulated.
32 devices in a mesh: old: 4 (over y, core), new: 8 (over z, x).
Axes of the slice: x: 2, y: 2, z: 4, core: 2. Of those that a mesh axis runs over, the one named last changes fastest.
Arguments:
- old_field: bfloat16 [3, 27, 98304], P(None, None, ('old', 'new')), may hold values from -6 to 6
- pair_dest: int32 [32768, 1], P(('old', 'new')), may hold values from 0 to 31; in each aligned block of 1024 rows (0 to 1023, 1024 to 2047, ...) at most 128 rows name the same one
- pair_new: int32 [32768], P(('old', 'new')), may hold values from 0 to 511
- pair_old: int32 [32768], P(('old', 'new')), may hold values from 0 to 3071
- pair_block: int32 [32768], P(('old', 'new')), may hold values from 0 to 3
- basis_old: bfloat16 [4, 27, 125], replicated, may hold values from -1.25 to 1.25
- basis_new: bfloat16 [4, 27, 125], replicated, may hold values from -0.5 to 0.5
- volume: float32 [2, 8, 1024], P(None, 'old', 'new'), may hold values from 0.25 to 36, as said below
Outputs:
- solution: float32 [3, 5, 16, 2048], P(None, None, 'old', 'new')
- residual: float32 [3, 5, 16, 2048], P(None, None, 'old', 'new')
Inputs may be any that keep to these rules, and one draw needn't show every extreme that they name: `pair_dest`: a device's index is its position along old times the number of devices along new plus its position along new; in each device's block of 1024 pairs at most 128 name one destination. `pair_new`: local element number (x * 2 + y) * 128 + z within the destination's block. `pair_old`: old element within the block of the device that holds the pair. `volume`: positive element factors.
All inputs are finite; a program needn't handle non-finite values.
Results may differ from a plain program's by a relative error of at most 0.003.
Values may be sent and summed in bfloat16 or wider, within the bound.
A program may use at most 64 MiB of HBM per device.

v0:
```python
import jax
import jax.numpy as jnp
import numpy as np
from jax import lax
from jax.sharding import PartitionSpec as P

ITERS = 4


LINE_MASS = np.array([[4.0, 2.0, -1.0], [2.0, 16.0, 2.0], [-1.0, 2.0, 4.0]]) / 15.0


def passed_along(shard, axis, by):
    size = lax.axis_size(axis)
    return lax.ppermute(shard, axis, [(i, (i + by) % size) for i in range(size)])


def split_axis(array, axis, count):
    moved = jnp.moveaxis(array, axis, -1)
    paired = moved[..., : 2 * count].reshape(moved.shape[:-1] + (count, 2))
    even_nodes = paired[..., 0]
    odd_nodes = paired[..., 1]
    after_nodes = jnp.concatenate(
        [even_nodes[..., 1:], moved[..., 2 * count : 2 * count + 1]], axis=-1
    )
    stacked = jnp.stack([even_nodes, odd_nodes, after_nodes], axis=0)
    return jnp.moveaxis(stacked, -1, axis + 1)


def pick_nodes(extended, cell_counts):
    along_first, along_second, along_third = cell_counts
    stacked = split_axis(extended, 3, along_third)
    stacked = split_axis(stacked, 3, along_second)
    stacked = split_axis(stacked, 3, along_first)
    return jnp.transpose(stacked, (3, 0, 1, 2, 4, 5, 6))


def merge_axis(array, local_axis, cell_axis):
    moved = jnp.moveaxis(array, (local_axis, cell_axis), (0, -1))
    count = moved.shape[-1]
    zero_pad = [(0, 0)] * (moved.ndim - 2)
    even_full = jnp.pad(moved[0], zero_pad + [(0, 1)]) + jnp.pad(moved[2], zero_pad + [(1, 0)])
    woven = jnp.stack([even_full[..., :count], moved[1]], axis=-1)
    woven = woven.reshape(woven.shape[:-2] + (2 * count,))
    return jnp.concatenate([woven, even_full[..., count:]], axis=-1)


def spread_nodes(element_nodes):
    summed = merge_axis(element_nodes, 3, 6)
    summed = merge_axis(summed, 2, 4)
    summed = merge_axis(summed, 1, 2)
    return jnp.transpose(summed, (0, 3, 2, 1))


def element_mass(element_nodes, volume):
    line_mass = jnp.asarray(LINE_MASS, dtype=jnp.float32)
    high = lax.Precision.HIGHEST
    applied = jnp.einsum("ia,cabdxyz->cibdxyz", line_mass, element_nodes, precision=high)
    applied = jnp.einsum("jb,cibdxyz->cijdxyz", line_mass, applied, precision=high)
    applied = jnp.einsum("kd,cijdxyz->cijkxyz", line_mass, applied, precision=high)
    return applied * volume


def fold_rims(assembled):
    front_face = passed_along(assembled[..., -1], "new", 1)
    inner_part = assembled[..., :-1]
    inner_part = jnp.concatenate(
        [inner_part[..., :1] + front_face[..., None], inner_part[..., 1:]], axis=3
    )
    side_face = passed_along(inner_part[:, :, -1, :], "old", 1)
    folded = inner_part[:, :, :-1]
    folded = jnp.concatenate(
        [folded[:, :, :1] + side_face[:, :, None, :], folded[:, :, 1:]], axis=2
    )
    return folded


def operate(vector, volume):
    upper_layer = passed_along(vector[..., 0], "new", -1)
    extended = jnp.concatenate([vector, upper_layer[..., None]], axis=3)
    upper_row = passed_along(extended[:, :, 0, :], "old", -1)
    extended = jnp.concatenate([extended, upper_row[:, :, None, :]], axis=2)
    element_nodes = pick_nodes(extended, volume.shape)
    return fold_rims(spread_nodes(element_mass(element_nodes, volume)))


def quadrature(coefficients, block_kind, basis_old, basis_new):
    summed = jnp.zeros(coefficients.shape, jnp.float32)
    for q in range(basis_old.shape[0]):
        chosen = jnp.where(
            (block_kind == q)[None, None, :], coefficients, jnp.zeros((), coefficients.dtype)
        )
        values = jnp.einsum(
            "cap,ak->ckp", chosen, basis_old[q], preferred_element_type=jnp.float32
        ).astype(jnp.bfloat16)
        summed = summed + jnp.einsum(
            "ckp,ak->cap", values, basis_new[q], preferred_element_type=jnp.float32
        )
    return summed


def squares(residual):
    return lax.psum(jnp.sum(residual * residual, axis=(1, 2, 3)), ("old", "new"))


def on_device(old_field, pair_dest, pair_new, pair_old, pair_block, basis_old, basis_new, volume):
    devices = lax.axis_size(("old", "new"))
    pair_count = pair_dest.shape[0]
    capacity = 4 * pair_count // devices
    cells_one, cells_two, cells_three = volume.shape
    elements = cells_one * cells_two * cells_three
    destination = pair_dest[:, 0]
    onehot = (destination[:, None] == jnp.arange(devices, dtype=jnp.int32)[None, :]).astype(
        jnp.int32
    )
    slot_rank = jnp.sum((jnp.cumsum(onehot, axis=0) - onehot) * onehot, axis=1)
    position = destination * capacity + slot_rank
    gathered = jnp.take(old_field, pair_old, axis=2)
    contribution = quadrature(gathered, pair_block, basis_old, basis_new)
    outgoing = (
        jnp.zeros((81, devices * capacity), jnp.float32)
        .at[:, position]
        .set(contribution.reshape(81, -1))
    )
    targets = jnp.full((devices * capacity,), elements, jnp.int32).at[position].set(pair_new)
    received, slot_element = (
        lax.all_to_all(
            outgoing.reshape(81, devices, capacity),
            ("old", "new"),
            split_axis=1,
            concat_axis=1,
            tiled=True,
        ),
        lax.all_to_all(
            targets.reshape(1, devices, capacity),
            ("old", "new"),
            split_axis=1,
            concat_axis=1,
            tiled=True,
        ),
    )
    arrived = received.reshape(81, -1)
    slot_element = slot_element.reshape(-1)
    element_load = (
        jnp.zeros((81, elements + 1), jnp.float32).at[:, slot_element].add(arrived)[:, :elements]
    )
    load_vector = fold_rims(
        spread_nodes(element_load.reshape(3, 3, 3, 3, cells_one, cells_two, cells_three))
    )
    solution = jnp.zeros_like(load_vector)
    residual = load_vector
    direction = load_vector
    norm_now = squares(residual)
    for iteration in range(ITERS):
        applied = operate(direction, volume)
        curvature = lax.psum(jnp.sum(direction * applied, axis=(1, 2, 3)), ("old", "new"))
        step_size = norm_now / curvature
        solution = solution + step_size[:, None, None, None] * direction
        residual = residual - step_size[:, None, None, None] * applied
        norm_next = squares(residual)
        direction = residual + (norm_next / norm_now)[:, None, None, None] * direction
        norm_now = norm_next
    return (solution, residual)


def solution(mesh):
    in_specs = (
        P(None, None, ("old", "new")),
        P(("old", "new"), None),
        P(("old", "new")),
        P(("old", "new")),
        P(("old", "new")),
        P(),
        P(),
        P(None, "old", "new"),
    )
    out_specs = (P(None, None, "old", "new"), P(None, None, "old", "new"))
    return jax.shard_map(
        on_device, mesh=mesh, in_specs=in_specs, out_specs=out_specs, check_vma=False
    )
```

profile of v0, /device:TPU:0, one launch (start us, length us, event | category | flops | bytes accessed | tf_op | source)
XLA Modules:
  0.0 579.1 jit_solution(5909297454449030575)
XLA Ops:
  1.3 9.0 %reduce-window.6 = s32[32,8,128]{2,1,0:T(8,128)S(1)} reduce-window(s32[32,8,128]{2,1,0:T(8,128)S(1)} %fusion.60, s32[]{:T(128)} %constant.17.clone.1), window={size=1x1x128 pad=0_0x0_0x127_0}, to_apply=%region_0.0 | reduce-window | flops 4161536 | bytes 262148 | tf_op jit(solution)/shard_map/reduce-window
  12.3 5.1 scatter_custom_fusion
  17.3 7.3 %all-to-all-start = ((s32[1,32,128]{2,0,1:T(1,128)}), s32[1,32,128]{2,0,1:T(1,128)S(1)}, u32[]{:S(2)}, u32[]{:S(2)}) async-start(s32[1,32,128]{2,0,1:T(1,128)} %bitcast.6), calls=%async_computation | async-start | bytes 32768 | tf_op jit(solution)/shard_map/all_to_all | solution.py:134
  26.1 4.5 copy.623
  31.3 7.5 %gather_fusion = bf16[1024,3,27]{2,1,0:T(4,128)(2,1)} fusion(bf16[3,27,3072]{1,0,2:T(4,128)(2,1)S(1)} %copy.623, s32[1024]{0:T(1024)S(1)} %fusion.106), kind=kCustom, calls=%fused_computation | custom fusion | bytes 335872 | tf_op jit(solution)/shard_map/jit(_take)/gather | solution.py:118
  38.9 9.2 %select_bitcast_fusion.3 = (bf16[3,27,1024]{1,0,2:T(4,128)(2,1)}, bf16[3,27,1024]{1,0,2:T(4,128)(2,1)S(1)}, bf16[3,27,1024]{1,0,2:T(4,128)(2,1)S(1)}, bf16[3,27,1024]{1,0,2:T(4,128)(2,1)S(1)}) fusion(pred[1024]{0:T(1024)(128)(4,1)S(1)} %get-tuple-element.120, bf16[1024,3,27]{2,1,0:T(4,128)(2,1)} %gather_fusion, pred[1024]{0:T(1024)(128)(4,1)S(1)} %get-tuple-element.126, ...), kind=kLoop, calls=%fused_computation.31 | loop fusion | flops 414720 | bytes 834560 | tf_op jit(solution)/shard_map/jit(_where)/select_n | solution.py:90
  55.1 3.8 scatter_custom_fusion.1
  60.6 5.8 %all-to-all-start.1 = ((f32[81,32,128]{2,0,1:T(8,128)}), f32[81,32,128]{2,0,1:T(8,128)S(1)}, u32[]{:S(2)}, u32[]{:S(2)}) async-start(f32[81,32,128]{2,0,1:T(8,128)} %copy.641), calls=%async_computation.1 | async-start | bytes 2883584 | tf_op jit(solution)/shard_map/all_to_all | solution.py:127
  67.1 35.3 %all-to-all-done.1 = f32[81,32,128]{2,0,1:T(8,128)S(1)} async-done(((f32[81,32,128]{2,0,1:T(8,128)}), f32[81,32,128]{2,0,1:T(8,128)S(1)}, u32[]{:S(2)}, u32[]{:S(2)}) %all-to-all-start.1) | async-done | bytes 1327136 | tf_op jit(solution)/shard_map/all_to_all | solution.py:127
  104.6 28.1 %scatter_custom_fusion.2 = f32[81,513]{0,1:T(8,128)S(1)} fusion(s32[4096]{0:T(1024)} %bitcast.616, f32[4096,81]{1,0:T(8,128)S(1)} %copy.643, f32[]{:T(128)} %constant.14.clone.1), kind=kCustom, calls=%fused_computation.113 | custom fusion | flops 331776 | bytes 166724 | tf_op jit(solution)/shard_map/scatter-add | solution.py:145
  133.4 4.3 copy.777
  137.6 6.2 %reshape.241 = f32[3,3,3,2,2,256]{5,4,3,0,1,2:T(2,128)S(1)} reshape(f32[3,3,3,2,2,128,2]{6,5,4,3,0,1,2:T(8,128)} %copy.777) | data formatting | bytes 221184 | tf_op jit(solution)/shard_map/reshape | solution.py:44
  144.8 6.3 %collective-permute-done = f32[3,5,5]{2,0,1:T(4,128)S(1)} collective-permute-done((f32[3,5,5]{2,0,1:T(4,128)S(1)}, f32[3,5,5]{2,0,1:T(4,128)S(1)}, u32[]{:S(2)}, u32[]{:S(2)}) %collective-permute-start) | collective-permute-done | bytes 332 | tf_op jit(solution)/shard_map/ppermute | solution.py:15
  169.5 4.3 copy.779
  173.8 6.2 %reshape.242 = f32[3,3,3,2,2,256]{5,4,3,0,1,2:T(2,128)S(1)} reshape(f32[3,3,3,2,2,128,2]{6,5,4,3,0,1,2:T(8,128)} %copy.779) | data formatting | bytes 221184 | tf_op jit(solution)/shard_map/reshape | solution.py:44
  181.0 6.3 %collective-permute-done.4 = f32[3,5,5]{2,0,1:T(4,128)S(1)} collective-permute-done((f32[3,5,5]{2,0,1:T(4,128)S(1)}, f32[3,5,5]{2,0,1:T(4,128)S(1)}, u32[]{:S(2)}, u32[]{:S(2)}) %collective-permute-start.4) | collective-permute-done | bytes 332 | tf_op jit(solution)/shard_map/ppermute | solution.py:15
  191.2 36.8 %all-reduce.30 = (f32[3]{0:T(128)S(1)}, f32[3]{0:T(128)S(1)}) all-reduce(f32[3]{0:T(128)S(1)} %get-tuple-element.7, f32[3]{0:T(128)S(1)} %get-tuple-element.6), channel_id=1, replica_groups=mesh['old'=4,'new'=8] {'old','new'}, use_global_device_ids=true, to_apply=%region_7.8 | all-reduce | flops 6 | bytes 48 | tf_op jit(solution)/shard_map/psum | solution.py:103
  228.2 40.9 %psum.58 = f32[3]{0:T(128)S(1)} all-reduce(f32[3]{0:T(128)S(1)} %get-tuple-element.20), channel_id=1, replica_groups=mesh['old'=4,'new'=8] {'old','new'}, use_global_device_ids=true, to_apply=%region_11.12 | all-reduce | flops 3 | bytes 24 | tf_op jit(solution)/shard_map/psum | solution.py:103
  285.0 4.3 copy.781
  289.3 6.2 %reshape.243 = f32[3,3,3,2,2,256]{5,4,3,0,1,2:T(2,128)S(1)} reshape(f32[3,3,3,2,2,128,2]{6,5,4,3,0,1,2:T(8,128)} %copy.781) | data formatting | bytes 221184 | tf_op jit(solution)/shard_map/reshape | solution.py:44
  298.7 4.3 collective-permute-done.8
  306.9 37.7 %psum.59 = f32[3]{0:T(128)S(1)} all-reduce(f32[3]{0:T(128)S(1)} %get-tuple-element.18), channel_id=1, replica_groups=mesh['old'=4,'new'=8] {'old','new'}, use_global_device_ids=true, to_apply=%region_13.14 | all-reduce | flops 3 | bytes 24 | tf_op jit(solution)/shard_map/psum | solution.py:156
  344.8 41.7 %psum.60 = f32[3]{0:T(128)S(1)} all-reduce(f32[3]{0:T(128)S(1)} %get-tuple-element.16), channel_id=1, replica_groups=mesh['old'=4,'new'=8] {'old','new'}, use_global_device_ids=true, to_apply=%region_15.16 | all-reduce | flops 3 | bytes 24 | tf_op jit(solution)/shard_map/psum | solution.py:103
  402.5 4.3 copy.783
  406.8 6.2 %reshape.244 = f32[3,3,3,2,2,256]{5,4,3,0,1,2:T(2,128)S(1)} reshape(f32[3,3,3,2,2,128,2]{6,5,4,3,0,1,2:T(8,128)} %copy.783) | data formatting | bytes 221184 | tf_op jit(solution)/shard_map/reshape | solution.py:44
  416.1 4.3 collective-permute-done.12
  424.3 36.9 %psum.61 = f32[3]{0:T(128)S(1)} all-reduce(f32[3]{0:T(128)S(1)} %get-tuple-element.14), channel_id=1, replica_groups=mesh['old'=4,'new'=8] {'old','new'}, use_global_device_ids=true, to_apply=%region_17.18 | all-reduce | flops 3 | bytes 24 | tf_op jit(solution)/shard_map/psum | solution.py:156
  461.4 41.8 %psum.62 = f32[3]{0:T(128)S(1)} all-reduce(f32[3]{0:T(128)S(1)} %get-tuple-element.12), channel_id=1, replica_groups=mesh['old'=4,'new'=8] {'old','new'}, use_global_device_ids=true, to_apply=%region_19.20 | all-reduce | flops 3 | bytes 24 | tf_op jit(solution)/shard_map/psum | solution.py:103
  519.2 4.3 copy.785
  523.5 6.2 %reshape.245 = f32[3,3,3,2,2,256]{5,4,3,0,1,2:T(2,128)S(1)} reshape(f32[3,3,3,2,2,128,2]{6,5,4,3,0,1,2:T(8,128)} %copy.785) | data formatting | bytes 221184 | tf_op jit(solution)/shard_map/reshape | solution.py:44
  532.8 4.3 collective-permute-done.16
  541.1 36.8 %psum.63 = f32[3]{0:T(128)S(1)} all-reduce(f32[3]{0:T(128)S(1)} %get-tuple-element.10), channel_id=1, replica_groups=mesh['old'=4,'new'=8] {'old','new'}, use_global_device_ids=true, to_apply=%region_21.22 | all-reduce | flops 3 | bytes 24 | tf_op jit(solution)/shard_map/psum | solution.py:156
  (365 shorter events, 109.6 us)
Async XLA Ops:
  10.8 19.8 %copy-start.2 = (bf16[4,27,125]{2,0,1:T(4,128)(2,1)S(1)}, bf16[4,27,125]{2,0,1:T(4,128)(2,1)}, u32[]{:S(2)}) copy-start(bf16[4,27,125]{2,0,1:T(4,128)(2,1)} %param.17) | copy-start | bytes 81004
  10.8 19.8 %copy-start.3 = (bf16[4,27,125]{2,0,1:T(4,128)(2,1)S(1)}, bf16[4,27,125]{2,0,1:T(4,128)(2,1)}, u32[]{:S(2)}) copy-start(bf16[4,27,125]{2,0,1:T(4,128)(2,1)} %param.18) | copy-start | bytes 81004
  12.3 13.1 %copy-start.5 = (s32[1024,1]{0,1:T(1,128)}, s32[1024,1]{0,1:T(1,128)S(1)}, u32[]{:S(2)}) copy-start(s32[1024,1]{0,1:T(1,128)S(1)} %compare_select_fusion.1) | copy-start | bytes 12292
  17.3 43.3 %all-to-all-start = ((s32[1,32,128]{2,0,1:T(1,128)}), s32[1,32,128]{2,0,1:T(1,128)S(1)}, u32[]{:S(2)}, u32[]{:S(2)}) async-start(s32[1,32,128]{2,0,1:T(1,128)} %bitcast.6), calls=%async_computation | async-start | bytes 32768 | tf_op jit(solution)/shard_map/all_to_all | solution.py:134
  49.5 3.7 copy-start
  60.6 41.7 %all-to-all-start.1 = ((f32[81,32,128]{2,0,1:T(8,128)}), f32[81,32,128]{2,0,1:T(8,128)S(1)}, u32[]{:S(2)}, u32[]{:S(2)}) async-start(f32[81,32,128]{2,0,1:T(8,128)} %copy.641), calls=%async_computation.1 | async-start | bytes 2883584 | tf_op jit(solution)/shard_map/all_to_all | solution.py:127
  144.7 6.4 %collective-permute-start = (f32[3,5,5]{2,0,1:T(4,128)S(1)}, f32[3,5,5]{2,0,1:T(4,128)S(1)}, u32[]{:S(2)}, u32[]{:S(2)}) collective-permute-start(f32[3,5,5]{2,0,1:T(4,128)S(1)} %bitcast.617), channel_id=1, source_target_pairs={{0,1},{1,2},{2,3},{3,4},{4,5},{5,6},{6,7},{7,0},{8,9},{9,10},{10,1... | collective-permute-start | bytes 908 | tf_op jit(solution)/shard_map/ppermute | solution.py:15
  151.4 3.3 collective-permute-start.1
  155.0 3.7 collective-permute-start.2
  158.8 1.6 collective-permute-start.3
  165.9 1.5 copy-start.1
  166.7 2.4 copy-start.4
  180.9 6.4 %collective-permute-start.4 = (f32[3,5,5]{2,0,1:T(4,128)S(1)}, f32[3,5,5]{2,0,1:T(4,128)S(1)}, u32[]{:S(2)}, u32[]{:S(2)}) collective-permute-start(f32[3,5,5]{2,0,1:T(4,128)S(1)} %bitcast.619), channel_id=1, source_target_pairs={{0,1},{1,2},{2,3},{3,4},{4,5},{5,6},{6,7},{7,0},{8,9},{9,10},{10,1... | collective-permute-start | bytes 908 | tf_op jit(solution)/shard_map/ppermute | solution.py:15
  187.6 3.3 collective-permute-start.5
  269.4 4.6 collective-permute-start.6
  274.2 1.8 collective-permute-start.7
  296.4 6.7 %collective-permute-start.8 = (f32[3,5,5]{2,0,1:T(4,128)S(1)}, f32[3,5,5]{2,0,1:T(4,128)S(1)}, u32[]{:S(2)}, u32[]{:S(2)}) collective-permute-start(f32[3,5,5]{2,0,1:T(4,128)S(1)} %bitcast.621), channel_id=1, source_target_pairs={{0,1},{1,2},{2,3},{3,4},{4,5},{5,6},{6,7},{7,0},{8,9},{9,10},{10,1... | collective-permute-start | bytes 908 | tf_op jit(solution)/shard_map/ppermute | solution.py:15
  303.4 3.3 collective-permute-start.9
  386.8 4.6 collective-permute-start.10
  391.6 1.8 collective-permute-start.11
  413.8 6.7 %collective-permute-start.12 = (f32[3,5,5]{2,0,1:T(4,128)S(1)}, f32[3,5,5]{2,0,1:T(4,128)S(1)}, u32[]{:S(2)}, u32[]{:S(2)}) collective-permute-start(f32[3,5,5]{2,0,1:T(4,128)S(1)} %bitcast.623), channel_id=1, source_target_pairs={{0,1},{1,2},{2,3},{3,4},{4,5},{5,6},{6,7},{7,0},{8,9},{9,10},{10,1... | collective-permute-start | bytes 908 | tf_op jit(solution)/shard_map/ppermute | solution.py:15
  420.8 3.3 collective-permute-start.13
  503.5 4.6 collective-permute-start.14
  508.3 1.9 collective-permute-start.15
  530.5 6.7 %collective-permute-start.16 = (f32[3,5,5]{2,0,1:T(4,128)S(1)}, f32[3,5,5]{2,0,1:T(4,128)S(1)}, u32[]{:S(2)}, u32[]{:S(2)}) collective-permute-start(f32[3,5,5]{2,0,1:T(4,128)S(1)} %bitcast.625), channel_id=1, source_target_pairs={{0,1},{1,2},{2,3},{3,4},{4,5},{5,6},{6,7},{7,0},{8,9},{9,10},{10,1... | collective-permute-start | bytes 908 | tf_op jit(solution)/shard_map/ppermute | solution.py:15
  537.5 3.3 collective-permute-start.17
where the time goes:
time: 589 us; the launch traced here: 579 us
  blocking collectives  273 us (46%)
  local copies, waits for them, and re-layouts  109 us (19%)
  waiting for transfers between devices  89.1 us (15%)
  other arithmetic  59.3 us (10%)
  starting transfers between devices  32.5 us (6%)
  matrix products  13.5 us (2%)
    psum x4, blocking collectives, squares(): lax.psum(jnp.sum(residual * residual, axis=(1, 2, 3)), ('old', 'new'))  161 us
    psum x3, blocking collectives, on_device(): lax.psum(jnp.sum(direction * applied, axis=(1, 2, 3)), ('old', 'new'))  111 us
    ppermute x18, waiting for transfers between devices, passed_along(): lax.ppermute(shard, axis, [(i, (i + by) % size) for i in range(size)])  53.8 us
    reshape x20, local copies, waits for them, and re-layouts, merge_axis(): woven = woven.reshape(woven.shape[:-2] + (2 * count,))  52.6 us
    all_to_all x1, waiting for transfers between devices, on_device(): lax.all_to_all(outgoing.reshape(81, devices, capacity), ('old', 'new'), s...  35.3 us
    scatter-add x1, other arithmetic, on_device(): jnp.zeros((81, elements + 1), jnp.float32).at[:, slot_element].add(arrived)  28.1 us
    ppermute x18, starting transfers between devices, passed_along(): lax.ppermute(shard, axis, [(i, (i + by) % size) for i in range(size)])  19.3 us
    unnamed x39, local copies, waits for them, and re-layouts  16.9 us
  transfers between devices with their start and end apart: 20, of which 19 were waited for; matrix products, arithmetic and copies ran while one was open for 6% of the time, Pallas kernels for 0%

commit v1 on v0

v1 whole, which is shorter than its diff:
```python
import functools
import math

import jax
import jax.numpy as jnp
from jax import lax
from jax.experimental import pallas as pl
from jax.experimental.pallas import tpu as pltpu
from jax.sharding import PartitionSpec as P

ITERS = 4
MESH = pl.DeviceIdType.MESH
VMEM = pltpu.VMEM
STRIDE = 32
ROWS = 3 * STRIDE
KINDS_AT = 27
F32 = jnp.float32
BF16 = jnp.bfloat16


def pack_kernel(devices, cap, dest_ref, new_ref, old_idx_ref, block_ref, field_ref, out_ref, square, rows, slots, count):
    lanes = rows.shape[1]
    old_elements = field_ref.shape[2]
    square[...] = jnp.zeros_like(square)

    def turn(j, carry):
        at = pl.ds(pl.multiple_of(j * lanes, lanes), lanes)
        for c in range(3):
            square[c * STRIDE : c * STRIDE + 27, :] = field_ref[c, :, at].astype(F32)
        rows[at, :] = square[...].T
        return carry

    lax.fori_loop(0, old_elements // lanes, turn, 0)
    slots[...] = jnp.zeros_like(slots)

    def clear(d, carry):
        count[d] = 0
        return carry

    lax.fori_loop(0, devices, clear, 0)
    lane = lax.broadcasted_iota(jnp.int32, (1, lanes), 1)

    def place(p, carry):
        d = dest_ref[p]
        rank = count[d]
        count[d] = rank + 1
        code = (new_ref[p] * 4 + block_ref[p]).astype(F32)
        row = rows[pl.ds(old_idx_ref[p], 1), :]
        slots[pl.ds(d * cap + rank, 1), :] = jnp.where(lane == KINDS_AT, code, row)
        return carry

    lax.fori_loop(0, dest_ref.shape[0], place, 0, unroll=8)

    row_at = lax.broadcasted_iota(jnp.int32, (ROWS, cap), 0)

    def send_form(d, carry):
        block = slots[pl.ds(pl.multiple_of(d * cap, cap), cap), :].T[:ROWS]
        code = block[KINDS_AT : KINDS_AT + 1].astype(jnp.int32)
        high = (code // 512).astype(F32)
        low = ((code // 4) % 128).astype(F32)
        kind = (code % 4).astype(F32)
        block = jnp.where(row_at == KINDS_AT, high, block)
        block = jnp.where(row_at == KINDS_AT + 1, low, block)
        block = jnp.where(row_at == KINDS_AT + 2, kind, block)
        out_ref[d] = block.astype(BF16)
        return carry

    lax.fori_loop(0, devices, send_form, 0)


def exchange_kernel(olds, news, cap, out_ref, in_ref, send_sem, recv_sem, own_sem):
    i, j = lax.axis_index("old"), lax.axis_index("new")
    me = i * news + j
    peers = [(a, b) for a in range(olds) for b in range(news) if a or b]
    barrier = pltpu.get_barrier_semaphore()
    for a, b in peers:
        pl.semaphore_signal(barrier, inc=1, device_id=((i + a) % olds, (j + b) % news), device_id_type=MESH)
    own_at = pl.ds(pl.multiple_of(me * cap, cap), cap)
    own = pltpu.make_async_copy(out_ref.at[me], in_ref.at[:, own_at], own_sem)
    own.start()
    pl.semaphore_wait(barrier, len(peers))
    copies = []
    for n, (a, b) in enumerate(peers):
        target = ((i + a) % olds, (j + b) % news)
        copy = pltpu.make_async_remote_copy(
            src_ref=out_ref.at[target[0] * news + target[1]],
            dst_ref=in_ref.at[:, own_at],
            send_sem=send_sem.at[n],
            recv_sem=recv_sem.at[n],
            device_id=target,
            device_id_type=MESH,
        )
        copy.start()
        copies.append(copy)
    own.wait()
    for copy in copies:
        copy.wait()


def row_of(big_x, a2, a3, c):
    return ((big_x * 3 + a2) * 3 + a3) * 3 + c


def load_kernel(cells, chunk, in_ref, old_ref, new_ref, volume_ref, pay_ref, square, first, second, total, load):
    kinds, _, points = old_ref.shape
    wide = square.shape[1] // 3
    elements = cells[0] * cells[1] * cells[2]
    for source in (old_ref, new_ref):
        square[...] = jnp.zeros_like(square)
        for q in range(kinds):
            for c in range(3):
                at = q * ROWS + c * STRIDE
                square[at : at + 27, c * wide : c * wide + points] = source[q].astype(F32)
        if source is old_ref:
            first[...] = square[...].T.astype(BF16)
        else:
            second[...] = square[...].astype(BF16)
    total[...] = jnp.zeros_like(total)

    def step(s, carry):
        at = pl.ds(pl.multiple_of(s * chunk, chunk), chunk)
        block = in_ref[:, at].astype(F32)
        kind = block[KINDS_AT + 2 : KINDS_AT + 3]
        element = (block[KINDS_AT : KINDS_AT + 1] * 128.0 + block[KINDS_AT + 1 : KINDS_AT + 2]).astype(jnp.int32)
        chosen = jnp.concatenate([jnp.where(kind == q, block, 0.0) for q in range(kinds)], axis=0).astype(BF16)
        values = jnp.dot(first[...], chosen, preferred_element_type=F32).astype(BF16)
        every = jnp.dot(second[...], values, preferred_element_type=F32)
        part = jnp.zeros((ROWS, chunk), F32)
        for q in range(kinds):
            part = part + jnp.where(kind == q, every[q * ROWS : (q + 1) * ROWS], 0.0)
        high = part.astype(BF16)
        low = (part - high.astype(F32)).astype(BF16)
        onehot = jnp.where(
            lax.broadcasted_iota(jnp.int32, (elements, chunk), 0) == element, 1.0, 0.0
        ).astype(BF16)
        total[...] += lax.dot_general(
            jnp.concatenate([high, low], axis=0), onehot, (((1,), (1,)), ((), ())), preferred_element_type=F32
        )
        return carry

    lax.fori_loop(0, in_ref.shape[1] // chunk, step, 0)
    load[...] = total[:ROWS] + total[ROWS:]
    for big_x in range(2 * cells[0] + 1):
        for a2 in range(3):
            for a3 in range(3):
                for c in range(3):
                    for y in range(cells[1]):
                        value = None
                        for x in range(cells[0]):
                            a1 = big_x - 2 * x
                            if 0 <= a1 <= 2:
                                r = c * STRIDE + a1 * 9 + a2 * 3 + a3
                                z = (x * cells[1] + y) * cells[2]
                                term = load[r : r + 1, z : z + cells[2]]
                                value = term if value is None else value + term
                        pay_ref[row_of(big_x, a2, a3, c), y : y + 1, :] = value
    for x in range(cells[0]):
        pay_ref[row_of(2 * cells[0] + 1, 0, 0, 0) + x] = volume_ref[x]


def line(a, b, c):
    ends = 2.0 * b
    return 4.0 * a + ends - c, 2.0 * (a + c) + 16.0 * b, 4.0 * c + ends - a


def solve_kernel(olds, news, cells, pay_ref, sol_ref, res_ref, around, volume, vec, prod, way, way_m, ans, parts, sums,
                 send_sem, recv_sem, sum_send, sum_recv):
    i, j = lax.axis_index("old"), lax.axis_index("new")
    cx, cy, cz = cells
    nodes_x = 2 * cx + 1
    ny = olds * cy
    volume_at = row_of(nodes_x, 0, 0, 0)
    near = [(a, b) for a in range(olds) for b in (0, 1, news - 1) if a or b]
    ring = [(0, b) for b in range(1, news)]
    barrier = pltpu.get_barrier_semaphore()
    greeted = near + [peer for peer in ring if peer not in near]
    for a, b in greeted:
        pl.semaphore_signal(barrier, inc=1, device_id=((i + a) % olds, (j + b) % news), device_id_type=MESH)
    around[i, 0] = pay_ref[...]
    pl.semaphore_wait(barrier, len(greeted))
    copies = []
    for n, (a, b) in enumerate(near):
        place = {0: 0, 1: 2, news - 1: 1}[b]
        copy = pltpu.make_async_remote_copy(
            src_ref=pay_ref,
            dst_ref=around.at[i, place],
            send_sem=send_sem.at[n],
            recv_sem=recv_sem.at[n],
            device_id=((i + a) % olds, (j + b) % news),
            device_id_type=MESH,
        )
        copy.start()
        copies.append(copy)
    for copy in copies:
        copy.wait()

    ghost_next = lax.broadcasted_iota(jnp.int32, (1, 1, cz), 2) < cz // 2

    def joined(first, count):
        pieces = []
        for a in range(olds):
            rows = pl.ds(first, count)
            ghost = jnp.where(ghost_next, around[a, 1, rows], around[a, 2, rows])
            pieces.append(jnp.concatenate([around[a, 0, rows], ghost], axis=2))
        return jnp.concatenate(pieces, axis=1)

    def up_y(v):
        return pltpu.roll(v, 1, v.ndim - 2)

    def up_z(v):
        return pltpu.roll(v, 1, v.ndim - 1)

    def down_y(v):
        return pltpu.roll(v, v.shape[-2] - 1, v.ndim - 2)

    def down_z(v):
        return pltpu.roll(v, v.shape[-1] - 1, v.ndim - 1)

    volume[...] = joined(volume_at, cx) * (1.0 / 3375.0)

    def assemble(big_x, carry):
        part = [[joined(row_of(big_x, a2, a3, 0), 3) for a3 in range(3)] for a2 in range(3)]
        flat = [[part[a2][0] + up_z(part[a2][2]), part[a2][1]] for a2 in range(3)]
        for q in range(2):
            vec[q, big_x] = flat[0][q] + up_y(flat[2][q])
            vec[2 + q, big_x] = flat[1][q]
        return carry

    lax.fori_loop(0, nodes_x, assemble, 0)

    def mass(c):
        gathered = {}

        def node(big_x, a2, a3):
            v = vec[(a2 % 2) * 2 + a3 % 2, big_x, c]
            if a2 == 2:
                v = down_y(v)
            if a3 == 2:
                v = down_z(v)
            return v

        for big_x in range(nodes_x):
            grid = [[node(big_x, a2, a3) for a3 in range(3)] for a2 in range(3)]
            grid = [line(*grid[a2]) for a2 in range(3)]
            grid = list(zip(*[line(grid[0][a3], grid[1][a3], grid[2][a3]) for a3 in range(3)]))
            gathered[big_x] = grid
        out = {}
        for a2 in range(3):
            for a3 in range(3):
                for x in range(cx):
                    ends = line(*[gathered[2 * x + a1][a2][a3] for a1 in range(3)])
                    for a1 in range(3):
                        term = ends[a1] * volume[x]
                        key = (2 * x + a1, a2, a3)
                        out[key] = out[key] + term if key in out else term
        for big_x in range(nodes_x):
            flat = [[out[big_x, a2, 0] + up_z(out[big_x, a2, 2]), out[big_x, a2, 1]] for a2 in range(3)]
            for q in range(2):
                prod[q, big_x, c] = flat[0][q] + up_y(flat[2][q])
                prod[2 + q, big_x, c] = flat[1][q]

    parts[...] = jnp.zeros_like(parts)
    norm_before, step_before = None, None
    for turn in range(ITERS):

        def apply(c, carry):
            mass(c)
            return carry

        lax.fori_loop(0, 3, apply, 0)
        for c in range(3):
            square = jnp.zeros((ny, cz), F32)
            cross = jnp.zeros((ny, cz), F32)
            for q in range(4):
                for big_x in range(nodes_x):
                    r = vec[q, big_x, c, :, :cz]
                    square = square + r * r
                    cross = cross + r * prod[q, big_x, c, :, :cz]
            parts[turn, c : c + 1, :] = jnp.sum(square, axis=0, keepdims=True)
            parts[turn, 3 + c : 4 + c, :] = jnp.sum(cross, axis=0, keepdims=True)
        copies = []
        for n, (a, b) in enumerate(ring):
            copy = pltpu.make_async_remote_copy(
                src_ref=parts.at[turn],
                dst_ref=sums.at[turn, j],
                send_sem=sum_send.at[turn, n],
                recv_sem=sum_recv.at[turn, n],
                device_id=(i, (j + b) % news),
                device_id_type=MESH,
            )
            copy.start()
            copies.append(copy)
        sums[turn, j] = parts[turn]
        for copy in copies:
            copy.wait()
        whole = sums[turn, 0]
        for b in range(1, news):
            whole = whole + sums[turn, b]
        whole = jnp.sum(whole, axis=1, keepdims=True)
        norm_now, cross_now = whole[0:3], whole[3:6]
        if turn == 0:
            step_size = norm_now / cross_now
            share = None
        else:
            share = norm_now / norm_before
            step_size = norm_now / (cross_now - share * norm_now / step_before)
        for c in range(3):
            alpha = step_size[c : c + 1]
            for q in range(4):
                for big_x in range(nodes_x):
                    at = (q, big_x, c)
                    r, w = vec[at], prod[at]
                    if turn > 0:
                        r_way = r + share[c : c + 1] * way[at]
                        w_way = w + share[c : c + 1] * way_m[at]
                        moved = ans[at] + alpha * r_way[:, :cz]
                    else:
                        r_way, w_way = r, w
                        moved = alpha * r[:, :cz]
                    way[at] = r_way
                    way_m[at] = w_way
                    ans[at] = moved
                    vec[at] = r - alpha * w_way
        norm_before, step_before = norm_now, step_size
    for source, target in ((ans, sol_ref), (vec, res_ref)):
        for a in range(olds):
            @pl.when(i == a)
            def _():
                target[...] = source[:, :, :, a * cy : (a + 1) * cy, :cz]


def on_device(olds, news, old_field, pair_dest, pair_new, pair_old, pair_block, basis_old, basis_new, volume):
    devices = olds * news
    pairs = pair_dest.shape[0]
    cap = 4 * pairs // devices
    cells = volume.shape
    elements = math.prod(cells)
    smem = pl.BlockSpec(memory_space=pltpu.SMEM)
    vmem = pl.BlockSpec(memory_space=VMEM)
    outgoing = pl.pallas_call(
        functools.partial(pack_kernel, devices, cap),
        out_shape=jax.ShapeDtypeStruct((devices, ROWS, cap), BF16),
        in_specs=[smem] * 4 + [vmem],
        out_specs=vmem,
        scratch_shapes=[
            VMEM((128, 128), F32),
            VMEM((old_field.shape[2], 128), F32),
            VMEM((devices * cap, 128), F32),
            pltpu.SMEM((devices,), jnp.int32),
        ],
        name="pack",
    )(pair_dest.reshape(-1), pair_new, pair_old, pair_block, old_field)
    arrived = pl.pallas_call(
        functools.partial(exchange_kernel, olds, news, cap),
        out_shape=jax.ShapeDtypeStruct((ROWS, devices * cap), BF16),
        in_specs=[vmem],
        out_specs=vmem,
        scratch_shapes=[
            pltpu.SemaphoreType.DMA((devices,)),
            pltpu.SemaphoreType.DMA((devices,)),
            pltpu.SemaphoreType.DMA,
        ],
        compiler_params=pltpu.CompilerParams(collective_id=0, has_side_effects=True),
        name="exchange",
    )(outgoing)
    kinds = basis_old.shape[0]
    wide = 128 * pl.cdiv(basis_old.shape[2], 128)
    chunk = 4 * 128
    pay_rows = row_of(2 * cells[0] + 1, 0, 0, 0) + cells[0]
    payload = pl.pallas_call(
        functools.partial(load_kernel, cells, chunk),
        out_shape=jax.ShapeDtypeStruct((pay_rows,) + cells[1:], F32),
        in_specs=[vmem] * 4,
        out_specs=vmem,
        scratch_shapes=[
            VMEM((kinds * ROWS, 3 * wide), F32),
            VMEM((3 * wide, kinds * ROWS), BF16),
            VMEM((kinds * ROWS, 3 * wide), BF16),
            VMEM((2 * ROWS, elements), F32),
            VMEM((ROWS, elements), F32),
        ],
        name="load",
    )(arrived, basis_old, basis_new, volume)
    nodes_x = 2 * cells[0] + 1
    ny, cz = olds * cells[1], cells[2]
    grid = (4, nodes_x, 3)
    own = jax.ShapeDtypeStruct(grid + cells[1:], F32)
    near = 3 * olds
    solved = pl.pallas_call(
        functools.partial(solve_kernel, olds, news, cells),
        out_shape=(own, own),
        in_specs=[vmem],
        out_specs=(vmem, vmem),
        scratch_shapes=[
            VMEM((olds, 3, pay_rows) + cells[1:], F32),
            VMEM((cells[0], ny, 2 * cz), F32),
            VMEM(grid + (ny, 2 * cz), F32),
            VMEM(grid + (ny, 2 * cz), F32),
            VMEM(grid + (ny, 2 * cz), F32),
            VMEM(grid + (ny, 2 * cz), F32),
            VMEM(grid + (ny, cz), F32),
            VMEM((ITERS, 8, cz), F32),
            VMEM((ITERS, news, 8, cz), F32),
            pltpu.SemaphoreType.DMA((near,)),
            pltpu.SemaphoreType.DMA((near,)),
            pltpu.SemaphoreType.DMA((ITERS, news)),
            pltpu.SemaphoreType.DMA((ITERS, news)),
        ],
        compiler_params=pltpu.CompilerParams(collective_id=1, has_side_effects=True),
        name="solve",
    )(payload)

    def woven(v):
        v = v.reshape((2, 2) + v.shape[1:])
        v = jnp.transpose(v, (3, 2, 4, 0, 5, 1))
        return v.reshape(3, nodes_x, 2 * cells[1], 2 * cz)

    return woven(solved[0]), woven(solved[1])


def solution(mesh):
    in_specs = (
        P(None, None, ("old", "new")),
        P(("old", "new"), None),
        P(("old", "new")),
        P(("old", "new")),
        P(("old", "new")),
        P(),
        P(),
        P(None, "old", "new"),
    )
    out_specs = (P(None, None, "old", "new"), P(None, None, "old", "new"))
    return jax.shard_map(
        functools.partial(on_device, mesh.shape["old"], mesh.shape["new"]),
        mesh=mesh,
        in_specs=in_specs,
        out_specs=out_specs,
        check_vma=False,
    )
```

time: 589 us -> 111 us (0.19); the launches traced: 579 us -> 111 us
  blocking collectives: 273 us -> 0 us
  Pallas kernels: 0 us -> 102 us
  local copies, waits for them, and re-layouts: 109 us -> 7.82 us
  waiting for transfers between devices: 89.1 us -> 0 us
  other arithmetic: 59.3 us -> 0 us
  starting transfers between devices: 32.5 us -> 0 us
  matrix products: 13.5 us -> 0 us
    psum x7 -> x0, blocking collectives: 273 us -> none  [the longest x4 161 us: squares(): lax.psum(jnp.sum(residual * residual, axis=(1, 2, 3)), ('old', 'new'))]
    pallas_call x0 -> x4, Pallas kernels: none -> 102 us  [the longest x1 53.5 us: on_device(): pl.pallas_call(functools.partial(solve_kernel, olds, news, cells), out_sh...]
    ppermute x18 -> x0, waiting for transfers between devices: 53.8 us -> none  [passed_along(): lax.ppermute(shard, axis, [(i, (i + by) % size) for i in range(size)])]
    reshape x26 -> x2, local copies, waits for them, and re-layouts: 55.6 us -> 2.89 us  [woven(): v = v.reshape((2, 2) + v.shape[1:])]
    all_to_all x2 -> x0, waiting for transfers between devices: 35.3 us -> none  [the longest x1 35.3 us: on_device(): lax.all_to_all(outgoing.reshape(81, devices, capacity), ('old', 'new'), s...]
    scatter-add x1 -> x0, other arithmetic: 28.1 us -> none  [on_device(): jnp.zeros((81, elements + 1), jnp.float32).at[:, slot_element].add(arrived)]
    ppermute x18 -> x0, starting transfers between devices: 19.3 us -> none  [passed_along(): lax.ppermute(shard, axis, [(i, (i + by) % size) for i in range(size)])]
    slice x92 -> x0, local copies, waits for them, and re-layouts: 17.3 us -> none  [the longest x12 10.5 us: split_axis(): odd_nodes = paired[..., 1]]
  transfers between devices with their start and end apart: 20 -> 0, of which waited for: 19 -> 0; matrix products, arithmetic and copies ran while one was open for 6% -> 0% of each run, Pallas kernels for 0% -> 0%
where the time goes in v1:
time: 111 us
  Pallas kernels  102 us (92%)
  local copies, waits for them, and re-layouts  7.82 us (7%)
    pallas_call x1, Pallas kernels, on_device(): pl.pallas_call(functools.partial(solve_kernel, olds, news, cells), out_sh...  53.5 us
    pallas_call x1, Pallas kernels, on_device(): pl.pallas_call(functools.partial(exchange_kernel, olds, news, cap), out_s...  26.4 us
    pallas_call x1, Pallas kernels, on_device(): pl.pallas_call(functools.partial(pack_kernel, devices, cap), out_shape=ja...  12.7 us
    pallas_call x1, Pallas kernels, on_device(): pl.pallas_call(functools.partial(load_kernel, cells, chunk), out_shape=ja...  9.74 us
    unnamed x6, local copies, waits for them, and re-layouts  4.93 us
    reshape x2, local copies, waits for them, and re-layouts, woven(): v = v.reshape((2, 2) + v.shape[1:])  2.89 us

profile of v1, /device:TPU:0, one launch (start us, length us, event | category | flops | bytes accessed | tf_op | source)
XLA Modules:
  0.0 110.8 jit_solution(17436773292830672263)
XLA Ops:
  0.6 1.4 %copy.14.old_ref = bf16[4,27,125]{2,1,0:T(8,128)(2,1)} copy(bf16[4,27,125]{2,0,1:T(4,128)(2,1)} %param.13) | data formatting | bytes 54000 | tf_op args[5]
  2.0 1.4 %copy.15.new_ref = bf16[4,27,125]{2,1,0:T(8,128)(2,1)} copy(bf16[4,27,125]{2,0,1:T(4,128)(2,1)} %param.14) | data formatting | bytes 54000 | tf_op args[6]
  3.4 12.7 %pack.1.out_ref = bf16[32,96,128]{2,1,0:T(8,128)(2,1)} custom-call(s32[1024]{0:T(1024)} %bitcast.13, s32[1024]{0:T(1024)} %new_ref.2, s32[1024]{0:T(1024)} %old_idx_ref.1, s32[1024]{0:T(1024)} %block_ref.1, bf16[3,27,3072]{2,1,0:T(8,128)(2,1)} %field_ref.1), custom_call_target="tpu_custom_call" | custom-call | tf_op jit(solution)/shard_map/pack/pallas_call | solution.py:340
  16.1 26.4 %exchange.1.in_ref = bf16[96,4096]{1,0:T(8,128)(2,1)} custom-call(bf16[32,96,128]{2,1,0:T(8,128)(2,1)} %pack.1.out_ref), custom_call_target="tpu_custom_call" | custom-call | tf_op jit(solution)/shard_map/exchange/pallas_call | solution.py:353
  42.5 9.7 %load.1.pay_ref = f32[137,2,128]{2,1,0:T(2,128)} custom-call(bf16[96,4096]{1,0:T(8,128)(2,1)} %exchange.1.in_ref, bf16[4,27,125]{2,1,0:T(8,128)(2,1)} %copy.14.old_ref, bf16[4,27,125]{2,1,0:T(8,128)(2,1)} %copy.15.new_ref, f32[2,2,128]{2,1,0:T(2,128)} %volume_ref.1), custom_call_target="tpu_custom_call" | custom-call | tf_op jit(solution)/shard_map/load/pallas_call | solution.py:370
  52.2 53.5 %solve.1 = (f32[4,5,3,2,128]{4,3,2,1,0:T(2,128)}, f32[4,5,3,2,128]{4,3,2,1,0:T(2,128)}) custom-call(f32[137,2,128]{2,1,0:T(2,128)} %load.1.pay_ref), custom_call_target="tpu_custom_call" | custom-call | tf_op jit(solution)/shard_map/solve/pallas_call | solution.py:389
  105.7 0.0 copy-start
  105.7 2.0 %copy.17 = f32[2,2,5,3,2,128]{2,1,5,0,4,3:T(2,128)S(1)} copy(f32[2,2,5,3,2,128]{5,4,3,2,1,0:T(2,128)} %bitcast.12) | data formatting | bytes 122880 | tf_op jit(solution)/shard_map/reshape | solution.py:414
  107.7 1.1 copy.19
  108.8 0.0 copy-done
  108.8 0.9 copy.16
  109.7 1.1 copy.18
Async XLA Ops:
  105.7 3.1 %copy-start = (f32[4,5,3,2,128]{4,3,2,1,0:T(2,128)S(1)}, f32[4,5,3,2,128]{4,3,2,1,0:T(2,128)}, u32[]{:S(2)}) copy-start(f32[4,5,3,2,128]{4,3,2,1,0:T(2,128)} %get-tuple-element.4) | copy-start | bytes 184324

commit v2 on v1

--- a/solution.py
+++ b/solution.py
@@ -8,11 +8,11 @@
 from jax.experimental.pallas import tpu as pltpu
 from jax.sharding import PartitionSpec as P
 
-ITERS = 4
 MESH = pl.DeviceIdType.MESH
 VMEM = pltpu.VMEM
 STRIDE = 32
 ROWS = 3 * STRIDE
+EDGE = 8
 KINDS_AT = 27
 F32 = jnp.float32
 BF16 = jnp.bfloat16
@@ -101,8 +101,8 @@
     return ((big_x * 3 + a2) * 3 + a3) * 3 + c
 
 
-def load_kernel(cells, chunk, in_ref, old_ref, new_ref, volume_ref, pay_ref, square, first, second, total, load):
-    kinds, _, points = old_ref.shape
+def load_kernel(cells, chunk, in_ref, old_ref, new_ref, volume_ref, pay_ref, edge_ref, square, first, second, total, load):
+    _, kinds, points = old_ref.shape
     wide = square.shape[1] // 3
     elements = cells[0] * cells[1] * cells[2]
     for source in (old_ref, new_ref):
@@ -110,7 +110,7 @@
         for q in range(kinds):
             for c in range(3):
                 at = q * ROWS + c * STRIDE
-                square[at : at + 27, c * wide : c * wide + points] = source[q].astype(F32)
+                square[at : at + 27, c * wide : c * wide + points] = source[:, q].astype(F32)
         if source is old_ref:
             first[...] = square[...].T.astype(BF16)
         else:
@@ -156,6 +156,19 @@
                         pay_ref[row_of(big_x, a2, a3, c), y : y + 1, :] = value
     for x in range(cells[0]):
         pay_ref[row_of(2 * cells[0] + 1, 0, 0, 0) + x] = volume_ref[x]
+    group, cz = edge_ref.shape[1], cells[2]
+    for r in range(row_of(2 * cells[0] + 1, 0, 0, 0) + cells[0], pay_ref.shape[0]):
+        pay_ref[r] = jnp.zeros(cells[1:], F32)
+    lane = lax.broadcasted_iota(jnp.int32, (1, 1, cz), 2)
+    first_cells = jnp.zeros(edge_ref.shape[1:], F32)
+    last_cells = jnp.zeros(edge_ref.shape[1:], F32)
+    for t in range(cz // EDGE):
+        rows = pay_ref[t * group : (t + 1) * group]
+        here = lane // EDGE == t
+        first_cells = jnp.where(here, pltpu.roll(rows, EDGE * t, 2), first_cells)
+        last_cells = jnp.where(here, pltpu.roll(rows, (EDGE * t + EDGE) % cz, 2), last_cells)
+    edge_ref[0] = first_cells
+    edge_ref[1] = last_cells
 
 
 def line(a, b, c):
@@ -163,27 +176,27 @@
     return 4.0 * a + ends - c, 2.0 * (a + c) + 16.0 * b, 4.0 * c + ends - a
 
 
-def solve_kernel(olds, news, cells, pay_ref, sol_ref, res_ref, around, volume, vec, prod, way, way_m, ans, parts, sums,
-                 send_sem, recv_sem, sum_send, sum_recv):
+def solve_kernel(olds, news, cells, pay_ref, edge_ref, sol_ref, res_ref, around, edges, ghost, volume, b0, b1, b2, b3, b4,
+                 ans, parts, sums, woven, send_sem, recv_sem, edge_send, edge_recv, sum_send, sum_recv):
     i, j = lax.axis_index("old"), lax.axis_index("new")
     cx, cy, cz = cells
     nodes_x = 2 * cx + 1
     ny = olds * cy
     volume_at = row_of(nodes_x, 0, 0, 0)
-    near = [(a, b) for a in range(olds) for b in (0, 1, news - 1) if a or b]
+    column = [(a, 0) for a in range(1, olds)]
+    sides = [(a, b) for b in (1, news - 1) for a in range(olds)]
     ring = [(0, b) for b in range(1, news)]
     barrier = pltpu.get_barrier_semaphore()
-    greeted = near + [peer for peer in ring if peer not in near]
+    greeted = column + sides + [peer for peer in ring if peer not in sides]
     for a, b in greeted:
         pl.semaphore_signal(barrier, inc=1, device_id=((i + a) % olds, (j + b) % news), device_id_type=MESH)
-    around[i, 0] = pay_ref[...]
+    around[0] = pay_ref[...]
     pl.semaphore_wait(barrier, len(greeted))
     copies = []
-    for n, (a, b) in enumerate(near):
-        place = {0: 0, 1: 2, news - 1: 1}[b]
+    for n, (a, b) in enumerate(column):
         copy = pltpu.make_async_remote_copy(
             src_ref=pay_ref,
-            dst_ref=around.at[i, place],
+            dst_ref=around.at[olds - a],
             send_sem=send_sem.at[n],
             recv_sem=recv_sem.at[n],
             device_id=((i + a) % olds, (j + b) % news),
@@ -191,18 +204,34 @@
         )
         copy.start()
         copies.append(copy)
+    for n, (a, b) in enumerate(sides):
+        side = 1 if b == 1 else 0
+        copy = pltpu.make_async_remote_copy(
+            src_ref=edge_ref.at[side],
+            dst_ref=edges.at[side, (olds - a) % olds],
+            send_sem=edge_send.at[n],
+            recv_sem=edge_recv.at[n],
+            device_id=((i + a) % olds, (j + b) % news),
+            device_id_type=MESH,
+        )
+        copy.start()
+        copies.append(copy)
     for copy in copies:
         copy.wait()
 
-    ghost_next = lax.broadcasted_iota(jnp.int32, (1, 1, cz), 2) < cz // 2
+    group = edge_ref.shape[1]
+    lane = lax.broadcasted_iota(jnp.int32, (1, 1, cz), 2)
+    after = jnp.concatenate([edges[0, a] for a in range(olds)], axis=1)
+    before = jnp.concatenate([edges[1, a] for a in range(olds)], axis=1)
+    for t in range(cz // EDGE):
+        first = pltpu.roll(after, (cz - EDGE * t) % cz, 2)
+        last = pltpu.roll(before, (2 * cz - EDGE - EDGE * t) % cz, 2)
+        ghost[t * group : (t + 1) * group] = jnp.where(lane < EDGE, first, jnp.where(lane >= cz - EDGE, last, 0.0))
 
     def joined(first, count):
-        pieces = []
-        for a in range(olds):
-            rows = pl.ds(first, count)
-            ghost = jnp.where(ghost_next, around[a, 1, rows], around[a, 2, rows])
-            pieces.append(jnp.concatenate([around[a, 0, rows], ghost], axis=2))
-        return jnp.concatenate(pieces, axis=1)
+        rows = pl.ds(first, count)
+        mine = jnp.concatenate([around[a, rows] for a in range(olds)], axis=1)
+        return jnp.concatenate([mine, ghost[rows]], axis=2)
 
     def up_y(v):
         return pltpu.roll(v, 1, v.ndim - 2)
@@ -222,62 +251,60 @@
         part = [[joined(row_of(big_x, a2, a3, 0), 3) for a3 in range(3)] for a2 in range(3)]
         flat = [[part[a2][0] + up_z(part[a2][2]), part[a2][1]] for a2 in range(3)]
         for q in range(2):
-            vec[q, big_x] = flat[0][q] + up_y(flat[2][q])
-            vec[2 + q, big_x] = flat[1][q]
+            b0[q, big_x] = flat[0][q] + up_y(flat[2][q])
+            b0[2 + q, big_x] = flat[1][q]
         return carry
 
     lax.fori_loop(0, nodes_x, assemble, 0)
 
-    def mass(c):
-        gathered = {}
-
-        def node(big_x, a2, a3):
-            v = vec[(a2 % 2) * 2 + a3 % 2, big_x, c]
-            if a2 == 2:
-                v = down_y(v)
-            if a3 == 2:
-                v = down_z(v)
-            return v
-
-        for big_x in range(nodes_x):
-            grid = [[node(big_x, a2, a3) for a3 in range(3)] for a2 in range(3)]
-            grid = [line(*grid[a2]) for a2 in range(3)]
-            grid = list(zip(*[line(grid[0][a3], grid[1][a3], grid[2][a3]) for a3 in range(3)]))
-            gathered[big_x] = grid
-        out = {}
-        for a2 in range(3):
-            for a3 in range(3):
-                for x in range(cx):
-                    ends = line(*[gathered[2 * x + a1][a2][a3] for a1 in range(3)])
-                    for a1 in range(3):
-                        term = ends[a1] * volume[x]
-                        key = (2 * x + a1, a2, a3)
-                        out[key] = out[key] + term if key in out else term
-        for big_x in range(nodes_x):
-            flat = [[out[big_x, a2, 0] + up_z(out[big_x, a2, 2]), out[big_x, a2, 1]] for a2 in range(3)]
-            for q in range(2):
-                prod[q, big_x, c] = flat[0][q] + up_y(flat[2][q])
-                prod[2 + q, big_x, c] = flat[1][q]
-
-    parts[...] = jnp.zeros_like(parts)
-    norm_before, step_before = None, None
-    for turn in range(ITERS):
-
-        def apply(c, carry):
-            mass(c)
+    def mass(source, target):
+        def component(c, carry):
+            gathered = {}
+
+            def node(big_x, a2, a3):
+                v = source[(a2 % 2) * 2 + a3 % 2, big_x, c]
+                if a2 == 2:
+                    v = down_y(v)
+                if a3 == 2:
+                    v = down_z(v)
+                return v
+
+            for big_x in range(nodes_x):
+                grid = [[node(big_x, a2, a3) for a3 in range(3)] for a2 in range(3)]
+                grid = [line(*grid[a2]) for a2 in range(3)]
+                grid = list(zip(*[line(grid[0][a3], grid[1][a3], grid[2][a3]) for a3 in range(3)]))
+                gathered[big_x] = grid
+            out = {}
+            for a2 in range(3):
+                for a3 in range(3):
+                    for x in range(cx):
+                        ends = line(*[gathered[2 * x + a1][a2][a3] for a1 in range(3)])
+                        for a1 in range(3):
+                            term = ends[a1] * volume[x]
+                            key = (2 * x + a1, a2, a3)
+                            out[key] = out[key] + term if key in out else term
+            for big_x in range(nodes_x):
+                flat = [[out[big_x, a2, 0] + up_z(out[big_x, a2, 2]), out[big_x, a2, 1]] for a2 in range(3)]
+                for q in range(2):
+                    target[q, big_x, c] = flat[0][q] + up_y(flat[2][q])
+                    target[2 + q, big_x, c] = flat[1][q]
             return carry
 
-        lax.fori_loop(0, 3, apply, 0)
+        lax.fori_loop(0, 3, component, 0)
+
+    def products(turn, pairs):
+        held = sorted({n for pair in pairs for n in pair})
+        buffers = (b0, b1, b2, b3, b4)
+        parts[turn] = jnp.zeros(parts.shape[1:], F32)
         for c in range(3):
-            square = jnp.zeros((ny, cz), F32)
-            cross = jnp.zeros((ny, cz), F32)
+            totals = [jnp.zeros((ny, cz), F32) for _ in pairs]
             for q in range(4):
                 for big_x in range(nodes_x):
-                    r = vec[q, big_x, c, :, :cz]
-                    square = square + r * r
-                    cross = cross + r * prod[q, big_x, c, :, :cz]
-            parts[turn, c : c + 1, :] = jnp.sum(square, axis=0, keepdims=True)
-            parts[turn, 3 + c : 4 + c, :] = jnp.sum(cross, axis=0, keepdims=True)
+                    v = {n: buffers[n][q, big_x, c, :, :cz] for n in held}
+                    totals = [t + v[m] * v[n] for t, (m, n) in zip(totals, pairs)]
+            for n, t in enumerate(totals):
+                row = 3 * n + c
+                parts[turn, row : row + 1, :] = jnp.sum(t, axis=0, keepdims=True)
         copies = []
         for n, (a, b) in enumerate(ring):
             copy = pltpu.make_async_remote_copy(
@@ -297,36 +324,68 @@
         for b in range(1, news):
             whole = whole + sums[turn, b]
         whole = jnp.sum(whole, axis=1, keepdims=True)
-        norm_now, cross_now = whole[0:3], whole[3:6]
-        if turn == 0:
-            step_size = norm_now / cross_now
-            share = None
-        else:
-            share = norm_now / norm_before
-            step_size = norm_now / (cross_now - share * norm_now / step_before)
+        return [whole[3 * n : 3 * n + 3] for n in range(len(pairs))]
+
+    every = [(q, big_x) for q in range(4) for big_x in range(nodes_x)]
+
+    mass(b0, b1)
+    mass(b1, b2)
+    g00, g01, g11, g12, g22 = products(0, [(0, 0), (0, 1), (1, 1), (1, 2), (2, 2)])
+    step0 = g00 / g01
+    norm1 = g00 - 2.0 * step0 * g01 + step0 * step0 * g11
+    share0 = 1.0 + norm1 / g00
+    step1 = norm1 / (share0 * share0 * g01 - 2.0 * share0 * step0 * g11 + step0 * step0 * g12)
+    e1, e2 = step0 + step1 * share0, step0 * step1
+    norm2 = (g00 - 2.0 * e1 * g01 + (e1 * e1 + 2.0 * e2) * g11 - 2.0 * e1 * e2 * g12 + e2 * e2 * g22)
+    share1 = norm2 / norm1
+    for c in range(3):
+        s = [v[c : c + 1] for v in (step0, step1, share0, share1, e1, e2)]
+        for q, big_x in every:
+            at = (q, big_x, c)
+            r, m1 = b0[at], b1[at]
+            way = s[2] * r - s[0] * m1
+            ans[at] = s[0] * r[:, :cz] + s[1] * way[:, :cz]
+            r = r - s[4] * m1 + s[5] * b2[at]
+            b0[at] = r
+            b1[at] = r + s[3] * way
+    mass(b1, b2)
+    mass(b2, b3)
+    mass(b0, b4)
+    rr, pm, rm, mm, rmr, mmm, rmm = products(1, [(0, 0), (1, 2), (0, 2), (2, 2), (0, 4), (2, 3), (0, 3)])
+    step2 = rr / pm
+    norm3 = rr - 2.0 * step2 * rm + step2 * step2 * mm
+    share2 = norm3 / rr
+    curve = (rmr + step2 * step2 * mmm + share2 * share2 * pm - 2.0 * step2 * rmm + 2.0 * share2 * rm
+             - 2.0 * step2 * share2 * mm)
+    step3 = norm3 / curve
+    for c in range(3):
+        s2, s3, h2 = (v[c : c + 1] for v in (step2, step3, share2))
+        for q, big_x in every:
+            at = (q, big_x, c, slice(None), slice(0, cz))
+            p, m = b1[at], b2[at]
+            r = b0[at] - s2 * m
+            way = r + h2 * p
+            ans[q, big_x, c] = ans[q, big_x, c] + s2 * p + s3 * way
+            b0[at] = r - s3 * (b4[at] - s2 * b3[at] + h2 * m)
+
+    span = 2 * cy
+    for o, source in enumerate((ans, b0)):
         for c in range(3):
-            alpha = step_size[c : c + 1]
-            for q in range(4):
-                for big_x in range(nodes_x):
-                    at = (q, big_x, c)
-                    r, w = vec[at], prod[at]
-                    if turn > 0:
-                        r_way = r + share[c : c + 1] * way[at]
-                        w_way = w + share[c : c + 1] * way_m[at]
-                        moved = ans[at] + alpha * r_way[:, :cz]
-                    else:
-                        r_way, w_way = r, w
-                        moved = alpha * r[:, :cz]
-                    way[at] = r_way
-                    way_m[at] = w_way
-                    ans[at] = moved
-                    vec[at] = r - alpha * w_way
-        norm_before, step_before = norm_now, step_size
-    for source, target in ((ans, sol_ref), (vec, res_ref)):
-        for a in range(olds):
-            @pl.when(i == a)
-            def _():
-                target[...] = source[:, :, :, a * cy : (a + 1) * cy, :cz]
+            for q, big_x in every:
+                for y in range(cy):
+                    row = ((o * 3 + c) * nodes_x + big_x) * span + 2 * y + q // 2
+                    z = (q % 2) * cz
+                    woven[row : row + 1, z : z + cz] = source[q, big_x, c, y : y + 1, :cz]
+    lines = lax.broadcasted_iota(jnp.int32, (2 * cz, 2 * cz), 0)
+    columns = lax.broadcasted_iota(jnp.int32, (2 * cz, 2 * cz), 1)
+    spot = jnp.where(lines < cz, 2 * lines, 2 * (lines - cz) + 1)
+    weave = jnp.where(spot == columns, 1.0, 0.0)
+    result = jnp.dot(woven[...], weave, precision=lax.Precision.HIGHEST, preferred_element_type=F32)
+    for o, target in enumerate((sol_ref, res_ref)):
+        for c in range(3):
+            for big_x in range(nodes_x):
+                row = ((o * 3 + c) * nodes_x + big_x) * span
+                target[c, big_x] = result[row : row + span]
 
 
 def on_device(olds, news, old_field, pair_dest, pair_new, pair_old, pair_block, basis_old, basis_new, volume):
@@ -366,12 +425,18 @@
     kinds = basis_old.shape[0]
     wide = 128 * pl.cdiv(basis_old.shape[2], 128)
     chunk = 4 * 128
-    pay_rows = row_of(2 * cells[0] + 1, 0, 0, 0) + cells[0]
-    payload = pl.pallas_call(
+    cz = cells[2]
+    groups = cz // EDGE
+    group = pl.cdiv(row_of(2 * cells[0] + 1, 0, 0, 0) + cells[0], groups)
+    pay_rows = groups * group
+    payload, edge = pl.pallas_call(
         functools.partial(load_kernel, cells, chunk),
-        out_shape=jax.ShapeDtypeStruct((pay_rows,) + cells[1:], F32),
+        out_shape=(
+            jax.ShapeDtypeStruct((pay_rows,) + cells[1:], F32),
+            jax.ShapeDtypeStruct((2, group) + cells[1:], F32),
+        ),
         in_specs=[vmem] * 4,
-        out_specs=vmem,
+        out_specs=(vmem, vmem),
         scratch_shapes=[
             VMEM((kinds * ROWS, 3 * wide), F32),
             VMEM((3 * wide, kinds * ROWS), BF16),
@@ -380,42 +445,38 @@
             VMEM((ROWS, elements), F32),
         ],
         name="load",
-    )(arrived, basis_old, basis_new, volume)
+    )(arrived, jnp.transpose(basis_old, (1, 0, 2)), jnp.transpose(basis_new, (1, 0, 2)), volume)
     nodes_x = 2 * cells[0] + 1
-    ny, cz = olds * cells[1], cells[2]
+    ny = olds * cells[1]
     grid = (4, nodes_x, 3)
-    own = jax.ShapeDtypeStruct(grid + cells[1:], F32)
-    near = 3 * olds
-    solved = pl.pallas_call(
+    own = jax.ShapeDtypeStruct((3, nodes_x, 2 * cells[1], 2 * cz), F32)
+    return pl.pallas_call(
         functools.partial(solve_kernel, olds, news, cells),
         out_shape=(own, own),
-        in_specs=[vmem],
+        in_specs=[vmem, vmem],
         out_specs=(vmem, vmem),
         scratch_shapes=[
-            VMEM((olds, 3, pay_rows) + cells[1:], F32),
+            VMEM((olds, pay_rows) + cells[1:], F32),
+            VMEM((2, olds, group) + cells[1:], F32),
+            VMEM((pay_rows, ny, cz), F32),
             VMEM((cells[0], ny, 2 * cz), F32),
-            VMEM(grid + (ny, 2 * cz), F32),
-            VMEM(grid + (ny, 2 * cz), F32),
-            VMEM(grid + (ny, 2 * cz), F32),
-            VMEM(grid + (ny, 2 * cz), F32),
+        ]
+        + [VMEM(grid + (ny, 2 * cz), F32)] * 5
+        + [
             VMEM(grid + (ny, cz), F32),
-            VMEM((ITERS, 8, cz), F32),
-            VMEM((ITERS, news, 8, cz), F32),
-            pltpu.SemaphoreType.DMA((near,)),
-            pltpu.SemaphoreType.DMA((near,)),
-            pltpu.SemaphoreType.DMA((ITERS, news)),
-            pltpu.SemaphoreType.DMA((ITERS, news)),
+            VMEM((2, 24, cz), F32),
+            VMEM((2, news, 24, cz), F32),
+            VMEM((2 * 3 * nodes_x * 2 * cells[1], 2 * cz), F32),
+            pltpu.SemaphoreType.DMA((olds,)),
+            pltpu.SemaphoreType.DMA((olds,)),
+            pltpu.SemaphoreType.DMA((2 * olds,)),
+            pltpu.SemaphoreType.DMA((2 * olds,)),
+            pltpu.SemaphoreType.DMA((2, news)),
+            pltpu.SemaphoreType.DMA((2, news)),
         ],
         compiler_params=pltpu.CompilerParams(collective_id=1, has_side_effects=True),
         name="solve",
-    )(payload)
-
-    def woven(v):
-        v = v.reshape((2, 2) + v.shape[1:])
-        v = jnp.transpose(v, (3, 2, 4, 0, 5, 1))
-        return v.reshape(3, nodes_x, 2 * cells[1], 2 * cz)
-
-    return woven(solved[0]), woven(solved[1])
+    )(payload, edge)
 
 
 def solution(mesh):

time: 111 us -> 82.5 us (0.74)
  Pallas kernels: 102 us -> 79.4 us
  local copies, waits for them, and re-layouts: 7.82 us -> 2.1 us
    pallas_call x1, Pallas kernels: 53.5 us -> 30.2 us  [on_device(): pl.pallas_call(functools.partial(solve_kernel, olds, news, cells), out_sh...]
    reshape x2 -> x0, local copies, waits for them, and re-layouts: 2.89 us -> none  [woven(): v = v.reshape((2, 2) + v.shape[1:])]
    unnamed x6 -> x4, local copies, waits for them, and re-layouts: 4.93 us -> 2.1 us
where the time goes in v2:
time: 82.5 us; the launch traced here: 82.2 us
  Pallas kernels  79.4 us (96%)
  local copies, waits for them, and re-layouts  2.1 us (3%)
    pallas_call x1, Pallas kernels, on_device(): pl.pallas_call(functools.partial(solve_kernel, olds, news, cells), out_sh...  30.2 us
    pallas_call x1, Pallas kernels, on_device(): pl.pallas_call(functools.partial(exchange_kernel, olds, news, cap), out_s...  26.4 us
    pallas_call x1, Pallas kernels, on_device(): pl.pallas_call(functools.partial(pack_kernel, devices, cap), out_shape=ja...  12.8 us
    pallas_call x1, Pallas kernels, on_device(): pl.pallas_call(functools.partial(load_kernel, cells, chunk), out_shape=(j...  10.1 us
    unnamed x4, local copies, waits for them, and re-layouts  2.1 us

profile of v2, /device:TPU:0, one launch (start us, length us, event | category | flops | bytes accessed | tf_op | source)
XLA Modules:
  0.0 82.2 jit_solution(4506755299470524446)
XLA Ops:
  0.6 12.8 %pack.1.out_ref = bf16[32,96,128]{2,1,0:T(8,128)(2,1)} custom-call(s32[1024]{0:T(1024)} %bitcast.5, s32[1024]{0:T(1024)} %new_ref.1, s32[1024]{0:T(1024)} %old_idx_ref.1, s32[1024]{0:T(1024)} %block_ref.1, bf16[3,27,3072]{2,1,0:T(8,128)(2,1)} %field_ref.1), custom_call_target="tpu_custom_call" | custom-call | tf_op jit(solution)/shard_map/pack/pallas_call | solution.py:399
  13.4 26.4 %exchange.1.in_ref = bf16[96,4096]{1,0:T(8,128)(2,1)} custom-call(bf16[32,96,128]{2,1,0:T(8,128)(2,1)} %pack.1.out_ref), custom_call_target="tpu_custom_call" | custom-call | tf_op jit(solution)/shard_map/exchange/pallas_call | solution.py:412
  39.8 10.1 %load.1 = (f32[144,2,128]{2,1,0:T(2,128)}, f32[2,9,2,128]{3,2,1,0:T(2,128)}) custom-call(bf16[96,4096]{1,0:T(8,128)(2,1)} %exchange.1.in_ref, bf16[27,4,125]{2,1,0:T(4,128)(2,1)} %bitcast.3, bf16[27,4,125]{2,1,0:T(4,128)(2,1)} %bitcast.4, f32[2,2,128]{2,1,0:T(2,128)} %volume_ref.1), custom_call_target="tpu_custom_call" | custom-call | tf_op jit(solution)/shard_map/load/pallas_call | solution.py:432
  49.8 30.2 %solve.1 = (f32[3,5,4,256]{3,2,1,0:T(4,128)}, f32[3,5,4,256]{3,2,1,0:T(4,128)}) custom-call(f32[144,2,128]{2,1,0:T(2,128)} %get-tuple-element.4.pay_ref, f32[2,9,2,128]{3,2,1,0:T(2,128)} %get-tuple-element.5.edge_ref), custom_call_target="tpu_custom_call" | custom-call | tf_op jit(solution)/shard_map/solve/pallas_call | solution.py:453
  80.1 0.0 copy-start
  80.1 1.5 %copy.12 = f32[3,5,4,256]{3,2,1,0:T(4,128)} copy(f32[3,5,4,256]{3,2,1,0:T(4,128)} %get-tuple-element.8) | data formatting | bytes 122880
  81.6 0.0 copy-done
  81.6 0.6 copy.13
Async XLA Ops:
  80.1 1.5 %copy-start = (f32[3,5,4,256]{3,2,1,0:T(4,128)S(1)}, f32[3,5,4,256]{3,2,1,0:T(4,128)}, u32[]{:S(2)}) copy-start(f32[3,5,4,256]{3,2,1,0:T(4,128)} %get-tuple-element.9) | copy-start | bytes 184324

commit v3 on v2

--- a/solution.py
+++ b/solution.py
@@ -21,16 +21,17 @@
 def pack_kernel(devices, cap, dest_ref, new_ref, old_idx_ref, block_ref, field_ref, out_ref, square, rows, slots, count):
     lanes = rows.shape[1]
     old_elements = field_ref.shape[2]
-    square[...] = jnp.zeros_like(square)
+    for c in range(3):
+        square[c * STRIDE : c * STRIDE + 27, :] = field_ref[c].astype(F32)
+        square[c * STRIDE + 27 : (c + 1) * STRIDE, :] = jnp.zeros((STRIDE - 27, old_elements), F32)
+    square[ROWS:, :] = jnp.zeros((lanes - ROWS, old_elements), F32)
 
     def turn(j, carry):
         at = pl.ds(pl.multiple_of(j * lanes, lanes), lanes)
-        for c in range(3):
-            square[c * STRIDE : c * STRIDE + 27, :] = field_ref[c, :, at].astype(F32)
-        rows[at, :] = square[...].T
-        return carry
-
-    lax.fori_loop(0, old_elements // lanes, turn, 0)
+        rows[at, :] = square[:, at].T
+        return carry
+
+    lax.fori_loop(0, old_elements // lanes, turn, 0, unroll=4)
     slots[...] = jnp.zeros_like(slots)
 
     def clear(d, carry):
@@ -65,26 +66,31 @@
         out_ref[d] = block.astype(BF16)
         return carry
 
-    lax.fori_loop(0, devices, send_form, 0)
-
-
-def exchange_kernel(olds, news, cap, out_ref, in_ref, send_sem, recv_sem, own_sem):
+    lax.fori_loop(0, devices, send_form, 0, unroll=4)
+
+
+def row_of(big_x, a2, a3, c):
+    return ((big_x * 3 + a2) * 3 + a3) * 3 + c
+
+
+def load_kernel(olds, news, cells, cap, together, out_ref, old_ref, new_ref, volume_ref, pay_ref, edge_ref, in_ref, square,
+                first, second, total, load, send_sem, recv_sem):
     i, j = lax.axis_index("old"), lax.axis_index("new")
-    me = i * news + j
-    peers = [(a, b) for a in range(olds) for b in range(news) if a or b]
+    peers = sorted(((a, b) for a in range(olds) for b in range(news) if a or b), key=lambda p: (abs(p[1] - news // 2), p))
+    place = {peer: n for n, peer in enumerate(peers + [(0, 0)])}
     barrier = pltpu.get_barrier_semaphore()
     for a, b in peers:
         pl.semaphore_signal(barrier, inc=1, device_id=((i + a) % olds, (j + b) % news), device_id_type=MESH)
-    own_at = pl.ds(pl.multiple_of(me * cap, cap), cap)
-    own = pltpu.make_async_copy(out_ref.at[me], in_ref.at[:, own_at], own_sem)
-    own.start()
+    n = place[0, 0]
+    pltpu.make_async_copy(out_ref.at[i * news + j], in_ref.at[:, n * cap : (n + 1) * cap], recv_sem.at[n]).start()
     pl.semaphore_wait(barrier, len(peers))
     copies = []
-    for n, (a, b) in enumerate(peers):
+    for a, b in peers:
         target = ((i + a) % olds, (j + b) % news)
+        n = place[(olds - a) % olds, (news - b) % news]
         copy = pltpu.make_async_remote_copy(
             src_ref=out_ref.at[target[0] * news + target[1]],
-            dst_ref=in_ref.at[:, own_at],
+            dst_ref=in_ref.at[:, n * cap : (n + 1) * cap],
             send_sem=send_sem.at[n],
             recv_sem=recv_sem.at[n],
             device_id=target,
@@ -92,16 +98,7 @@
         )
         copy.start()
         copies.append(copy)
-    own.wait()
-    for copy in copies:
-        copy.wait()
-
-
-def row_of(big_x, a2, a3, c):
-    return ((big_x * 3 + a2) * 3 + a3) * 3 + c
-
-
-def load_kernel(cells, chunk, in_ref, old_ref, new_ref, volume_ref, pay_ref, edge_ref, square, first, second, total, load):
+    chunk = together * cap
     _, kinds, points = old_ref.shape
     wide = square.shape[1] // 3
     elements = cells[0] * cells[1] * cells[2]
@@ -118,6 +115,9 @@
     total[...] = jnp.zeros_like(total)
 
     def step(s, carry):
+        for n in range(together):
+            spot = pl.ds(pl.multiple_of(s * chunk + n * cap, cap), cap)
+            pltpu.make_async_copy(out_ref.at[0], in_ref.at[:, spot], recv_sem.at[s * together + n]).wait()
         at = pl.ds(pl.multiple_of(s * chunk, chunk), chunk)
         block = in_ref[:, at].astype(F32)
         kind = block[KINDS_AT + 2 : KINDS_AT + 3]
@@ -169,6 +169,8 @@
         last_cells = jnp.where(here, pltpu.roll(rows, (EDGE * t + EDGE) % cz, 2), last_cells)
     edge_ref[0] = first_cells
     edge_ref[1] = last_cells
+    for copy in copies:
+        copy.wait_send()
 
 
 def line(a, b, c):
@@ -402,35 +404,22 @@
         in_specs=[smem] * 4 + [vmem],
         out_specs=vmem,
         scratch_shapes=[
-            VMEM((128, 128), F32),
+            VMEM((128, old_field.shape[2]), F32),
             VMEM((old_field.shape[2], 128), F32),
             VMEM((devices * cap, 128), F32),
             pltpu.SMEM((devices,), jnp.int32),
         ],
         name="pack",
     )(pair_dest.reshape(-1), pair_new, pair_old, pair_block, old_field)
-    arrived = pl.pallas_call(
-        functools.partial(exchange_kernel, olds, news, cap),
-        out_shape=jax.ShapeDtypeStruct((ROWS, devices * cap), BF16),
-        in_specs=[vmem],
-        out_specs=vmem,
-        scratch_shapes=[
-            pltpu.SemaphoreType.DMA((devices,)),
-            pltpu.SemaphoreType.DMA((devices,)),
-            pltpu.SemaphoreType.DMA,
-        ],
-        compiler_params=pltpu.CompilerParams(collective_id=0, has_side_effects=True),
-        name="exchange",
-    )(outgoing)
     kinds = basis_old.shape[0]
     wide = 128 * pl.cdiv(basis_old.shape[2], 128)
-    chunk = 4 * 128
+    together = 4
     cz = cells[2]
     groups = cz // EDGE
     group = pl.cdiv(row_of(2 * cells[0] + 1, 0, 0, 0) + cells[0], groups)
     pay_rows = groups * group
     payload, edge = pl.pallas_call(
-        functools.partial(load_kernel, cells, chunk),
+        functools.partial(load_kernel, olds, news, cells, cap, together),
         out_shape=(
             jax.ShapeDtypeStruct((pay_rows,) + cells[1:], F32),
             jax.ShapeDtypeStruct((2, group) + cells[1:], F32),
@@ -438,14 +427,18 @@
         in_specs=[vmem] * 4,
         out_specs=(vmem, vmem),
         scratch_shapes=[
+            VMEM((ROWS, devices * cap), BF16),
             VMEM((kinds * ROWS, 3 * wide), F32),
             VMEM((3 * wide, kinds * ROWS), BF16),
             VMEM((kinds * ROWS, 3 * wide), BF16),
             VMEM((2 * ROWS, elements), F32),
             VMEM((ROWS, elements), F32),
+            pltpu.SemaphoreType.DMA((devices,)),
+            pltpu.SemaphoreType.DMA((devices,)),
         ],
+        compiler_params=pltpu.CompilerParams(collective_id=0, has_side_effects=True),
         name="load",
-    )(arrived, jnp.transpose(basis_old, (1, 0, 2)), jnp.transpose(basis_new, (1, 0, 2)), volume)
+    )(outgoing, jnp.transpose(basis_old, (1, 0, 2)), jnp.transpose(basis_new, (1, 0, 2)), volume)
     nodes_x = 2 * cells[0] + 1
     ny = olds * cells[1]
     grid = (4, nodes_x, 3)

time: 82.5 us -> 73.9 us (0.90)
  Pallas kernels: 79.4 us -> 70.9 us
    pallas_call x2 -> x1, Pallas kernels: 36.5 us -> 32.1 us  [on_device(): pl.pallas_call(functools.partial(load_kernel, olds, news, cells, cap, tog...]
    pallas_call x1, Pallas kernels: 12.8 us -> 9.18 us  [on_device(): pl.pallas_call(functools.partial(pack_kernel, devices, cap), out_shape=ja...]
where the time goes in v3:
time: 73.9 us; the launch traced here: 73.6 us
  Pallas kernels  70.9 us (96%)
  local copies, waits for them, and re-layouts  2.1 us (3%)
    pallas_call x1, Pallas kernels, on_device(): pl.pallas_call(functools.partial(load_kernel, olds, news, cells, cap, tog...  32.1 us
    pallas_call x1, Pallas kernels, on_device(): pl.pallas_call(functools.partial(solve_kernel, olds, news, cells), out_sh...  29.6 us
    pallas_call x1, Pallas kernels, on_device(): pl.pallas_call(functools.partial(pack_kernel, devices, cap), out_shape=ja...  9.18 us
    unnamed x4, local copies, waits for them, and re-layouts  2.1 us

profile of v3, /device:TPU:0, one launch (start us, length us, event | category | flops | bytes accessed | tf_op | source)
XLA Modules:
  0.0 73.6 jit_solution(11466113631672834062)
XLA Ops:
  0.6 9.2 %pack.1.out_ref = bf16[32,96,128]{2,1,0:T(8,128)(2,1)} custom-call(s32[1024]{0:T(1024)} %bitcast.5, s32[1024]{0:T(1024)} %new_ref.1, s32[1024]{0:T(1024)} %old_idx_ref.1, s32[1024]{0:T(1024)} %block_ref.1, bf16[3,27,3072]{2,1,0:T(8,128)(2,1)} %field_ref.1), custom_call_target="tpu_custom_call" | custom-call | tf_op jit(solution)/shard_map/pack/pallas_call | solution.py:401
  9.8 32.1 %load.1 = (f32[144,2,128]{2,1,0:T(2,128)}, f32[2,9,2,128]{3,2,1,0:T(2,128)}) custom-call(bf16[32,96,128]{2,1,0:T(8,128)(2,1)} %pack.1.out_ref, bf16[27,4,125]{2,1,0:T(4,128)(2,1)} %bitcast.3, bf16[27,4,125]{2,1,0:T(4,128)(2,1)} %bitcast.4, f32[2,2,128]{2,1,0:T(2,128)} %volume_ref.1), custom_call_target="tpu_custom_call" | custom-call | tf_op jit(solution)/shard_map/load/pallas_call | solution.py:421
  41.9 29.6 %solve.1 = (f32[3,5,4,256]{3,2,1,0:T(4,128)}, f32[3,5,4,256]{3,2,1,0:T(4,128)}) custom-call(f32[144,2,128]{2,1,0:T(2,128)} %get-tuple-element.4.pay_ref, f32[2,9,2,128]{3,2,1,0:T(2,128)} %get-tuple-element.5.edge_ref), custom_call_target="tpu_custom_call" | custom-call | tf_op jit(solution)/shard_map/solve/pallas_call | solution.py:446
  71.5 0.0 copy-start
  71.5 1.5 %copy.12 = f32[3,5,4,256]{3,2,1,0:T(4,128)} copy(f32[3,5,4,256]{3,2,1,0:T(4,128)} %get-tuple-element.8) | data formatting | bytes 122880
  73.0 0.0 copy-done
  73.0 0.6 copy.13
Async XLA Ops:
  71.5 1.5 %copy-start = (f32[3,5,4,256]{3,2,1,0:T(4,128)S(1)}, f32[3,5,4,256]{3,2,1,0:T(4,128)}, u32[]{:S(2)}) copy-start(f32[3,5,4,256]{3,2,1,0:T(4,128)} %get-tuple-element.9) | copy-start | bytes 184324

commit v4 on v3

--- a/solution.py
+++ b/solution.py
@@ -50,7 +50,7 @@
         slots[pl.ds(d * cap + rank, 1), :] = jnp.where(lane == KINDS_AT, code, row)
         return carry
 
-    lax.fori_loop(0, dest_ref.shape[0], place, 0, unroll=8)
+    lax.fori_loop(0, dest_ref.shape[0], place, 0, unroll=16)
 
     row_at = lax.broadcasted_iota(jnp.int32, (ROWS, cap), 0)
 
@@ -195,17 +195,24 @@
     around[0] = pay_ref[...]
     pl.semaphore_wait(barrier, len(greeted))
     copies = []
-    for n, (a, b) in enumerate(column):
+
+    def layers_to(source, spot, target, n):
         copy = pltpu.make_async_remote_copy(
-            src_ref=pay_ref,
-            dst_ref=around.at[olds - a],
+            src_ref=source,
+            dst_ref=around.at[spot],
             send_sem=send_sem.at[n],
             recv_sem=recv_sem.at[n],
-            device_id=((i + a) % olds, (j + b) % news),
+            device_id=(target, j),
             device_id_type=MESH,
         )
         copy.start()
-        copies.append(copy)
+        return copy
+
+    half = olds // 2
+    partner = i + 1 - 2 * (i % 2)
+    ahead = olds + 2 * (i % 2) - 1
+    direct = [layers_to(pay_ref, olds - 2 * k, (i + 2 * k) % olds, k - 1) for k in range(1, half)]
+    copies.append(layers_to(pay_ref, ahead % olds, partner, half - 1))
     for n, (a, b) in enumerate(sides):
         side = 1 if b == 1 else 0
         copy = pltpu.make_async_remote_copy(
@@ -218,6 +225,11 @@
         )
         copy.start()
         copies.append(copy)
+    for k, copy in enumerate(direct, start=1):
+        copy.wait_recv()
+        copies.append(layers_to(around.at[olds - 2 * k], (ahead - 2 * k) % olds, partner, half - 1 + k))
+    for copy in direct:
+        copy.wait_send()
     for copy in copies:
         copy.wait()
 

time: 73.9 us -> 72.5 us (0.981)
  Pallas kernels: 70.9 us -> 69.5 us
    pallas_call x1, Pallas kernels: 29.6 us -> 28.5 us  [on_device(): pl.pallas_call(functools.partial(solve_kernel, olds, news, cells), out_sh...]
where the time goes in v4:
time: 72.5 us; the launch traced here: 72.3 us
  Pallas kernels  69.5 us (96%)
  local copies, waits for them, and re-layouts  2.1 us (3%)
    pallas_call x1, Pallas kernels, on_device(): pl.pallas_call(functools.partial(load_kernel, olds, news, cells, cap, tog...  32.1 us
    pallas_call x1, Pallas kernels, on_device(): pl.pallas_call(functools.partial(solve_kernel, olds, news, cells), out_sh...  28.5 us
    pallas_call x1, Pallas kernels, on_device(): pl.pallas_call(functools.partial(pack_kernel, devices, cap), out_shape=ja...  8.91 us
    unnamed x4, local copies, waits for them, and re-layouts  2.1 us

profile of v4, /device:TPU:0, one launch (start us, length us, event | category | flops | bytes accessed | tf_op | source)
XLA Modules:
  0.0 72.3 jit_solution(8756162629393398791)
XLA Ops:
  0.6 8.9 %pack.1.out_ref = bf16[32,96,128]{2,1,0:T(8,128)(2,1)} custom-call(s32[1024]{0:T(1024)} %bitcast.5, s32[1024]{0:T(1024)} %new_ref.1, s32[1024]{0:T(1024)} %old_idx_ref.1, s32[1024]{0:T(1024)} %block_ref.1, bf16[3,27,3072]{2,1,0:T(8,128)(2,1)} %field_ref.1), custom_call_target="tpu_custom_call" | custom-call | tf_op jit(solution)/shard_map/pack/pallas_call | solution.py:413
  9.5 32.1 %load.1 = (f32[144,2,128]{2,1,0:T(2,128)}, f32[2,9,2,128]{3,2,1,0:T(2,128)}) custom-call(bf16[32,96,128]{2,1,0:T(8,128)(2,1)} %pack.1.out_ref, bf16[27,4,125]{2,1,0:T(4,128)(2,1)} %bitcast.3, bf16[27,4,125]{2,1,0:T(4,128)(2,1)} %bitcast.4, f32[2,2,128]{2,1,0:T(2,128)} %volume_ref.1), custom_call_target="tpu_custom_call" | custom-call | tf_op jit(solution)/shard_map/load/pallas_call | solution.py:433
  41.7 28.5 %solve.1 = (f32[3,5,4,256]{3,2,1,0:T(4,128)}, f32[3,5,4,256]{3,2,1,0:T(4,128)}) custom-call(f32[144,2,128]{2,1,0:T(2,128)} %get-tuple-element.4.pay_ref, f32[2,9,2,128]{3,2,1,0:T(2,128)} %get-tuple-element.5.edge_ref), custom_call_target="tpu_custom_call" | custom-call | tf_op jit(solution)/shard_map/solve/pallas_call | solution.py:458
  70.2 0.0 copy-start
  70.2 1.5 %copy.12 = f32[3,5,4,256]{3,2,1,0:T(4,128)} copy(f32[3,5,4,256]{3,2,1,0:T(4,128)} %get-tuple-element.8) | data formatting | bytes 122880
  71.7 0.0 copy-done
  71.7 0.6 copy.13
Async XLA Ops:
  70.2 1.5 %copy-start = (f32[3,5,4,256]{3,2,1,0:T(4,128)S(1)}, f32[3,5,4,256]{3,2,1,0:T(4,128)}, u32[]{:S(2)}) copy-start(f32[3,5,4,256]{3,2,1,0:T(4,128)} %get-tuple-element.9) | copy-start | bytes 184324
